TPU v7x, 512 devices: a whole 4x4x16 slice. The times are simulated.
512 devices in a mesh: occ: 16 (over y, z_hi), vir: 32 (over x, z_lo, core).
Axes of the slice: x: 4, y: 4, z: 16 (z_hi: 4, z_lo: 4; z = z_hi * 4 + z_lo), core: 2. Of those that a mesh axis runs over, the one named last changes fastest.
Arguments:
- amplitudes: float32 [4, 1024, 1024], P(None, 'occ', 'vir'), may hold values from -6 to 6
- integrals: float32 [4, 28672, 1024], P(None, 'vir', 'occ'), may hold values from -0.1875 to 0.1875
Outputs:
- ladder: float32 [4, 1024, 28672], P(None, 'occ', 'vir')
All inputs are finite; a program needn't handle non-finite values.
Results may differ from a plain program's by a relative error of at most 0.000073.
Values sent between devices are 32-bit elements; how exact they have to be, the bound alone decides.
A program may use at most 64 MiB of HBM per device.

v0:
```python
import jax
import jax.numpy as jnp
from jax import lax
from jax.sharding import PartitionSpec as P


def contract_block(left, piece):
    return lax.dot_general(
        left,
        piece,
        (((2,), (2,)), ((0,), (0,))),
        precision=lax.Precision.HIGHEST,
        preferred_element_type=jnp.float32,
    )


def body(amplitudes, integrals):
    gathered = lax.all_gather(amplitudes, "vir", axis=2, tiled=True)
    panel_sum = contract_block(gathered, lax.all_gather(integrals, "occ", axis=2, tiled=True))
    return 0.5 * panel_sum


def solution(mesh):
    in_specs = (P(None, "occ", "vir"), P(None, "vir", "occ"))
    out_specs = P(None, "occ", "vir")
    return jax.shard_map(body, mesh=mesh, in_specs=in_specs, out_specs=out_specs, check_vma=False)
```

profile of v0, /device:TPU:9, one launch (start us, length us, event | category | flops | bytes accessed | tf_op | source)
XLA Modules:
  0.0 446.1 jit_solution(8332519620568645044)
XLA Ops:
  6.5 0.0 all-gather.3.cloned.1.call-start
  6.5 0.7 all-gather.3.cloned.1.call-update
  7.3 0.0 all-gather.5.cloned.1.call-start
  7.3 0.7 all-gather.5.cloned.1.call-update
  8.0 71.1 %all-gather.3.cloned.1.call-done = f32[4,64,1024]{1,2,0:T(8,128)} async-done(((f32[4,64,32]{1,2,0:T(8,128)}), f32[4,64,1024]{1,2,0:T(8,128)}) %all-gather.3.cloned.1.call-update) | async-done | bytes 1048592 | tf_op jit(solution)/shard_map/all_gather | solution.py:18
  79.1 347.4 %all-gather.5.cloned.1.call-done = f32[4,896,1024]{1,2,0:T(8,128)} async-done(((f32[4,896,64]{1,2,0:T(8,128)}), f32[4,896,1024]{1,2,0:T(8,128)}) %all-gather.5.cloned.1.call-update) | async-done | bytes 14680080 | tf_op jit(solution)/shard_map/all_gather | solution.py:19
  426.6 12.7 %convolution_multiply_fusion = f32[4,64,896]{2,1,0:T(8,128)} fusion(f32[4,64,1024]{1,2,0:T(8,128)} %all-gather.3.cloned.1.call-done, f32[4,896,1024]{1,2,0:T(8,128)} %all-gather.5.cloned.1.call-done), kind=kOutput, calls=%fused_computation | convolution fusion | flops 2818801664 | bytes 16646144 | tf_op jit(solution)/shard_map/dot_general | solution.py:8
Async XLA Ops:
  6.5 72.6 %all-gather.3.cloned.1.call-start = ((), (), s32[]{:S(2)}) async-start(), calls=%async_computation | async-start | bytes 2162688 | tf_op jit(solution)/shard_map/all_gather | solution.py:18
  7.3 419.3 %all-gather.5.cloned.1.call-start = ((), (), s32[]{:S(2)}) async-start(), calls=%async_computation.1 | async-start | bytes 15597568 | tf_op jit(solution)/shard_map/all_gather | solution.py:19
Sparse Core Ops, SparseCore 0:
  9.5 69.5 all-gather.2
  82.1 344.3 all-gather.4
where the time goes:
time: 446 us
  waiting for transfers between devices  420 us (94%)
  between operations  13.4 us (3%)
  matrix products  12.7 us (3%)
    all_gather x1, waiting for transfers between devices, body(): lax.all_gather(integrals, 'occ', axis=2, tiled=True)  347 us
    all_gather x1, waiting for transfers between devices, body(): gathered = lax.all_gather(amplitudes, 'vir', axis=2, tiled=True)  71.1 us
    dot_general x1, matrix products, contract_block(): lax.dot_general(left, piece, (((2,), (2,)), ((0,), (0,))), precision=lax....  12.7 us
  transfers between devices with their start and end apart: 2, of which 2 were waited for; matrix products, arithmetic and copies ran while one was open for 0% of the time, Pallas kernels for 0%

commit v1 on v0

--- a/solution.py
+++ b/solution.py
@@ -15,7 +15,9 @@
 
 
 def body(amplitudes, integrals):
-    gathered = lax.all_gather(amplitudes, "vir", axis=2, tiled=True)
+    gathered = jnp.concatenate(
+        lax.all_to_all(jnp.stack([amplitudes] * lax.axis_size("vir")), "vir", 0, 0), axis=2
+    )
     panel_sum = contract_block(gathered, lax.all_gather(integrals, "occ", axis=2, tiled=True))
     return 0.5 * panel_sum
 

time: 446 us -> 387 us (0.87)
  waiting for transfers between devices: 420 us -> 277 us
  blocking collectives: 0 us -> 77.4 us
    all_to_all x0 -> x1, blocking collectives: none -> 77.4 us  [body(): lax.all_to_all(jnp.stack([amplitudes] * lax.axis_size('vir')), 'vir', 0, 0)]
    all_gather x1, waiting for transfers between devices: 347 us -> 276 us  [body(): lax.all_gather(integrals, 'occ', axis=2, tiled=True)]
    all_gather x1 -> x0, waiting for transfers between devices: 71.1 us -> none  [body(): gathered = lax.all_gather(amplitudes, 'vir', axis=2, tiled=True)]
  transfers between devices with their start and end apart: 2 -> 1, of which waited for: 2 -> 1; matrix products, arithmetic and copies ran while one was open for 0% -> 2% of each run, Pallas kernels for 0% -> 0%
where the time goes in v1:
time: 387 us
  waiting for transfers between devices  277 us (72%)
  blocking collectives  77.4 us (20%)
  between operations  13.4 us (3%)
  matrix products  12.4 us (3%)
    all_gather x1, waiting for transfers between devices, body(): lax.all_gather(integrals, 'occ', axis=2, tiled=True)  276 us
    all_to_all x1, blocking collectives, body(): lax.all_to_all(jnp.stack([amplitudes] * lax.axis_size('vir')), 'vir', 0, 0)  77.4 us
    dot_general x1, matrix products, contract_block(): lax.dot_general(left, piece, (((2,), (2,)), ((0,), (0,))), precision=lax....  12.4 us
  transfers between devices with their start and end apart: 1, of which 1 were waited for; matrix products, arithmetic and copies ran while one was open for 2% of the time, Pallas kernels for 0%

profile of v1, /device:TPU:9, one launch (start us, length us, event | category | flops | bytes accessed | tf_op | source)
XLA Modules:
  0.0 386.5 jit_solution(5843839390117461624)
XLA Ops:
  6.5 0.0 copy-start
  6.5 0.0 all-gather.2.cloned.1.call-start
  6.5 0.7 all-gather.2.cloned.1.call-update
  7.3 0.1 copy-done
  7.4 0.2 broadcast_bitcast_fusion
  7.6 1.3 reshape.10
  8.9 77.4 %all_to_all.5 = f32[32,1,8192]{2,1,0:T(1,128)S(1)} all-to-all(f32[32,1,8192]{2,1,0:T(1,128)S(1)} %reshape.10), channel_id=1, replica_groups=mesh['occ'=16,'vir'=32] {'vir'}, dimensions={0} | all-to-all | bytes 2097152 | tf_op jit(solution)/shard_map/all_to_all | solution.py:19
  86.4 0.5 broadcast.2
  86.9 3.2 reduce
  90.1 0.8 reshape.11
  90.9 0.2 bitcast_bitcast_fusion
  91.2 0.2 copy.5
  91.4 276.0 %all-gather.2.cloned.1.call-done = f32[4,896,1024]{1,2,0:T(8,128)} async-done(((f32[4,896,64]{1,2,0:T(8,128)}), f32[4,896,1024]{1,2,0:T(8,128)}) %all-gather.2.cloned.1.call-update) | async-done | bytes 14680080 | tf_op jit(solution)/shard_map/all_gather | solution.py:21
  367.3 12.4 %convolution_multiply_fusion = f32[4,64,896]{2,1,0:T(8,128)} fusion(f32[4,64,1024]{1,2,0:T(8,128)S(1)} %bitcast.9, f32[4,896,1024]{1,2,0:T(8,128)} %all-gather.2.cloned.1.call-done), kind=kOutput, calls=%fused_computation | convolution fusion | flops 2818801664 | bytes 16646144 | tf_op jit(solution)/shard_map/dot_general | solution.py:8
Async XLA Ops:
  6.5 0.8 copy-start
  6.5 360.8 %all-gather.2.cloned.1.call-start = ((), (), s32[]{:S(2)}) async-start(), calls=%async_computation.1 | async-start | bytes 15597568 | tf_op jit(solution)/shard_map/all_gather | solution.py:21
Sparse Core Ops, SparseCore 0:
  10.3 356.9 all-gather.1
